TPU v7x, 128 devices: a whole 4x4x4 slice. The times are simulated.
128 devices in a mesh: comp: 2 (over z_hi), mr: 64 (over z_lo, y, x, core).
Axes of the slice: x: 4, y: 4, z: 4 (z_hi: 2, z_lo: 2; z = z_hi * 2 + z_lo), core: 2. Of those that a mesh axis runs over, the one named last changes fastest.
Arguments:
- spectrum: float32 [2, 1024, 2, 64, 512], P('comp', 'mr'), may hold values from -6 to 6
- radial_basis: bfloat16 [1024, 1024, 512], P('mr'), may hold values from -0.25 to 0.25
- cutoff: int32 [1024], P('mr'), may hold values from 128 to 512, as said below
- couplings: float32 [2, 2], replicated, may hold values from 0.5 to 1.5
- trap_potential: float32 [1024], replicated, may hold values from 0 to 2
- weights: float32 [1024], replicated, may hold values from 0.25 to 0.75
Outputs:
- evolved: float32 [2, 1024, 2, 64, 512], P('comp', 'mr')
Inputs may be any that keep to these rules, and one draw needn't show every extreme that they name: cutoff[m] is the number of Laguerre degrees kept for angular mode m; degrees from cutoff[m] on are dropped.
All inputs are finite; a program needn't handle non-finite values.
Results may differ from a plain program's by a relative error of at most 0.0089.
Values may be sent and summed in bfloat16 or wider, within the bound.
A program may use at most 128 MiB of HBM per device.

v0:
```python
import math
import jax
import jax.numpy as jnp
from jax import lax
from jax.sharding import PartitionSpec as P

TIMESTEP = 0.5
ROTATION = 0.7


def spectral_tables(mode_total):
    ordinal = jnp.arange(mode_total, dtype=jnp.int32)
    product = ordinal[:, None] * ordinal[None, :] % mode_total
    angles = product.astype(jnp.float32) * (2.0 * math.pi / mode_total)
    normalizer = 1.0 / math.sqrt(mode_total)
    return (
        (jnp.cos(angles) * normalizer).astype(jnp.bfloat16),
        (jnp.sin(angles) * normalizer).astype(jnp.bfloat16),
    )


def rotate(real_part, imag_part, phase_angle):
    cosine = jnp.cos(phase_angle)
    sine_value = jnp.sin(phase_angle)
    return (
        real_part * cosine + imag_part * sine_value,
        imag_part * cosine - real_part * sine_value,
    )


def forward_modes(cosine_table, sine_table, radial, planes):
    cosine_term = jnp.einsum(
        "am,rmk->rak", cosine_table, radial, preferred_element_type=jnp.float32
    )
    sine_term = jnp.einsum("am,rmk->rak", sine_table, radial, preferred_element_type=jnp.float32)
    real_part = cosine_term[..., :planes] - sine_term[..., planes:]
    imag_part = sine_term[..., :planes] + cosine_term[..., planes:]
    return (real_part, imag_part)


def inverse_modes(cosine_table, sine_table, kicked, planes):
    cosine_back = jnp.einsum(
        "am,rak->rmk", cosine_table, kicked, preferred_element_type=jnp.float32
    )
    sine_back = jnp.einsum("am,rak->rmk", sine_table, kicked, preferred_element_type=jnp.float32)
    back_real = cosine_back[..., :planes] + sine_back[..., planes:]
    back_imag = cosine_back[..., planes:] - sine_back[..., :planes]
    return jnp.concatenate([back_real, back_imag], -1)


def on_device(spectrum, radial_basis, cutoff, couplings, trap_potential, weights):
    local_modes = spectrum.shape[1]
    planes = spectrum.shape[3]
    degrees = spectrum.shape[4]
    radius_count = radial_basis.shape[1]
    mode_width = lax.axis_size("mr")
    mode_total = local_modes * mode_width
    first_mode = lax.axis_index("mr") * local_modes
    mode_ids = first_mode + jnp.arange(local_modes, dtype=jnp.int32)
    signed = jnp.where(mode_ids < mode_total // 2, mode_ids, mode_ids - mode_total).astype(
        jnp.float32
    )
    degree_ids = jnp.arange(degrees, dtype=jnp.int32)
    energy = (
        2.0 * degree_ids.astype(jnp.float32)[None, :]
        + (jnp.abs(signed) + 1.0 - ROTATION * signed)[:, None]
    )
    kinetic_phase = TIMESTEP * energy
    kept_mask = (degree_ids[None, :] < cutoff[:, None]).astype(jnp.float32)
    spin_real, spin_imag = rotate(spectrum[0, :, 0], spectrum[0, :, 1], kinetic_phase[:, None, :])
    coeffs = jnp.concatenate(
        [spin_real * kept_mask[:, None, :], spin_imag * kept_mask[:, None, :]], axis=1
    ).astype(jnp.bfloat16)
    synthesized = jnp.einsum(
        "mkn,mrn->rmk", coeffs, radial_basis, preferred_element_type=jnp.float32
    ).astype(jnp.bfloat16)
    cosine_table, sine_table = spectral_tables(mode_total)
    comp_width = lax.axis_size("comp")
    row_count = radius_count // (mode_width * comp_width)
    first_row = (lax.axis_index("comp") * mode_width + lax.axis_index("mr")) * row_count
    trap_rows = lax.dynamic_slice_in_dim(trap_potential, first_row, row_count)
    weight_rows = lax.dynamic_slice_in_dim(weights, first_row, row_count)
    everyone = ("comp", "mr")
    radial = lax.all_to_all(synthesized, everyone, split_axis=0, concat_axis=1, tiled=True)
    radial = radial.reshape(row_count * comp_width, mode_total, 2 * planes)
    real_part, imag_part = forward_modes(cosine_table, sine_table, radial, planes)
    density = (real_part * real_part + imag_part * imag_part).reshape(
        row_count, comp_width, mode_total, planes
    )
    phase_angle = TIMESTEP * (
        couplings[:, 0][None, :, None, None] * density
        + couplings[:, 1][None, :, None, None] * density[:, ::-1]
        + trap_rows[:, None, None, None]
    )
    kick_real, kick_imag = rotate(real_part, imag_part, phase_angle.reshape(real_part.shape))
    kicked = jnp.concatenate([kick_real, kick_imag], -1).astype(jnp.bfloat16)
    back = inverse_modes(cosine_table, sine_table, kicked, planes)
    back = back.reshape(row_count, comp_width * mode_total, 2 * planes)
    analysis_input = (back * weight_rows[:, None, None]).astype(jnp.bfloat16)
    gathered_modes = lax.all_to_all(
        analysis_input, everyone, split_axis=1, concat_axis=0, tiled=True
    )
    evolved = (
        jnp.einsum("rmk,mrn->mkn", gathered_modes, radial_basis, preferred_element_type=jnp.float32)
        * kept_mask[:, None, :]
    )
    return evolved.reshape(1, local_modes, 2, planes, degrees)


def solution(mesh):
    in_specs = (P("comp", "mr", None, None, None), P("mr", None, None), P("mr"), P(), P(), P())
    out_specs = P("comp", "mr", None, None, None)
    return jax.shard_map(
        on_device, mesh=mesh, in_specs=in_specs, out_specs=out_specs, check_vma=False
    )
```

profile of v0, /device:TPU:1, one launch (start us, length us, event | category | flops | bytes accessed | tf_op | source)
XLA Modules:
  0.0 319.5 jit_solution(5036196517199933014)
XLA Ops:
  0.0 0.7 fusion.34
  0.7 0.2 fusion.33
  0.9 3.0 fusion.22
  4.0 17.4 %convert_bitcast_fusion = bf16[1024,16,128]{0,2,1:T(8,128)(2,1)} fusion(bf16[16,1024,512]{2,1,0:T(8,128)(2,1)} %param.7, bf16[16,64,512]{2,1,0:T(8,128)(2,1)S(1)} %get-tuple-element.12, bf16[16,64,512]{2,1,0:T(8,128)(2,1)S(1)} %get-tuple-element.11), kind=kOutput, calls=%fused_computation.30 | convolution fusion | flops 2153775104 | bytes 23068672 | tf_op jit(solution)/shard_map/mkn,mrn->rmk/dot_general | solution.py:74
  21.3 6.9 %copy.20 = bf16[1024,16,128]{2,1,0:T(8,128)(2,1)} copy(bf16[1024,16,128]{0,2,1:T(8,128)(2,1)} %convert_bitcast_fusion) | data formatting | bytes 8388608 | tf_op jit(solution)/shard_map/convert_element_type | solution.py:76
  28.2 0.0 copy-start.2
  28.2 12.4 %all-to-all-start = ((bf16[1024,16,128]{2,1,0:T(8,128)(2,1)}), bf16[1024,16,128]{2,1,0:T(8,128)(2,1)}, u32[]{:S(2)}, u32[]{:S(2)}) async-start(bf16[1024,16,128]{2,1,0:T(8,128)(2,1)} %copy.20), calls=%async_computation | async-start | bytes 8388608 | tf_op jit(solution)/shard_map/all_to_all | solution.py:84
  40.7 0.8 dynamic_slice.6
  41.4 0.8 dynamic_slice.7
  42.2 0.0 copy-done.2
  42.2 0.2 slice_reduce_fusion.1
  42.4 50.7 %all-to-all-done = bf16[1024,16,128]{2,1,0:T(8,128)(2,1)} async-done(((bf16[1024,16,128]{2,1,0:T(8,128)(2,1)}), bf16[1024,16,128]{2,1,0:T(8,128)(2,1)}, u32[]{:S(2)}, u32[]{:S(2)}) %all-to-all-start) | async-done | bytes 4194336 | tf_op jit(solution)/shard_map/all_to_all | solution.py:84
  93.1 2.9 copy.21
  96.1 21.4 %convolution_bitcast_fusion.2 = f32[16,1024,128]{1,2,0:T(8,128)S(1)} fusion(bf16[16,1024,128]{2,1,0:T(8,128)(2,1)S(1)} %bitcast.85), kind=kOutput, calls=%fused_computation.34 | convolution fusion | flops 4311744512 | bytes 12582912 | tf_op jit(solution)/shard_map/am,rmk->rak/dot_general | solution.py:35
  117.4 21.3 %convolution_bitcast_fusion.3 = f32[16,1024,128]{1,2,0:T(8,128)S(1)} fusion(bf16[16,1024,128]{2,1,0:T(8,128)(2,1)S(1)} %bitcast.86), kind=kOutput, calls=%fused_computation.35 | convolution fusion | flops 4311744512 | bytes 12582912 | tf_op jit(solution)/shard_map/am,rmk->rak/dot_general | solution.py:32
  138.8 2.5 multiply_add_fusion
  141.3 15.3 %fusion.14 = (f32[8,2,1024,64]{2,3,1,0:T(8,128)S(1)}, f32[8,2,1024,64]{2,3,1,0:T(8,128)S(1)}) fusion(f32[8,2,1024,64]{2,3,1,0:T(8,128)S(1)} %bitcast.83, f32[8]{0:T(128)S(1)} %dynamic_slice.6, f32[2]{0:T(128)S(1)} %get-tuple-element.6, f32[2]{0:T(128)S(1)} %get-tuple-element.5), kind=kLoop, calls=%fused_computation.37 | loop fusion | flops 5242880 | bytes 12582960 | tf_op jit(solution)/shard_map/cos | solution.py:23
  156.6 5.4 %fusion.5 = (bf16[16,1024,64]{1,2,0:T(8,128)(2,1)}, bf16[16,1024,64]{1,2,0:T(8,128)(2,1)}) fusion(f32[8,2,1024,64]{2,3,1,0:T(8,128)S(1)} %get-tuple-element.14, f32[8,2,1024,64]{2,3,1,0:T(8,128)S(1)} %get-tuple-element.13, f32[16,1024,128]{1,2,0:T(8,128)S(1)} %convolution_bitcast_fusion.2, f32[16,1024,128]{1,2,0:T(8,128)S(1)} %convolution_bitcast_fusion.3), kind=kLoop, calls=%fused_computation.17 | loop fusion | flops 10485760 | bytes 29360128 | tf_op jit(solution)/shard_map/convert
  162.0 0.0 copy-start
  162.0 0.0 copy-start.1
  162.0 23.7 %convolution_bitcast_fusion = f32[16,1024,128]{1,2,0:T(8,128)} fusion(bf16[16,1024,64]{1,2,0:T(8,128)(2,1)} %get-tuple-element.8, bf16[16,1024,64]{1,2,0:T(8,128)(2,1)} %get-tuple-element.7), kind=kOutput, calls=%fused_computation.32 | convolution fusion | flops 4320133120 | bytes 12582912 | tf_op jit(solution)/shard_map/am,rak->rmk/dot_general | solution.py:45
  185.7 0.0 copy-done
  185.7 0.0 copy-done.1
  185.7 21.5 %convolution_bitcast_fusion.1 = f32[16,1024,128]{1,2,0:T(8,128)} fusion(bf16[16,1024,64]{1,2,0:T(8,128)(2,1)S(1)} %copy-done.1, bf16[16,1024,64]{1,2,0:T(8,128)(2,1)S(1)} %copy-done), kind=kOutput, calls=%fused_computation.33 | convolution fusion | flops 4320133120 | bytes 12582912 | tf_op jit(solution)/shard_map/am,rak->rmk/dot_general | solution.py:42
  207.2 10.5 %slice_add_fusion = (f32[16,1024,64]{1,2,0:T(8,128)S(1)}, f32[16,1024,64]{1,2,0:T(8,128)}) fusion(f32[16,1024,128]{1,2,0:T(8,128)} %convolution_bitcast_fusion, f32[16,1024,128]{1,2,0:T(8,128)} %convolution_bitcast_fusion.1), kind=kLoop, calls=%fused_computation.10 | loop fusion | flops 2097152 | bytes 25165824 | tf_op jit(solution)/shard_map/add | solution.py:46
  217.7 6.8 %pad_maximum_fusion = f32[16,1024,128]{1,2,0:T(8,128)} fusion(f32[16,1024,64]{1,2,0:T(8,128)} %get-tuple-element.10, f32[16,1024,64]{1,2,0:T(8,128)S(1)} %get-tuple-element.9), kind=kLoop, calls=%fused_computation | loop fusion | flops 2097152 | bytes 16777216 | tf_op jit(solution)/shard_map/concatenate | solution.py:48
  224.5 9.2 %copy.24 = f32[16,1024,128]{2,1,0:T(8,128)} copy(f32[16,1024,128]{1,2,0:T(8,128)} %pad_maximum_fusion) | data formatting | bytes 16777216 | tf_op jit(solution)/shard_map/concatenate | solution.py:48
  233.8 4.1 %fusion = bf16[8,2048,128]{2,1,0:T(8,128)(2,1)S(1)} fusion(f32[8]{0:T(128)S(1)} %dynamic_slice.7, f32[8,2048,128]{2,1,0:T(8,128)} %bitcast.81), kind=kLoop, calls=%fused_computation.2 | loop fusion | flops 4194304 | bytes 12582944 | tf_op jit(solution)/shard_map/convert_element_type | solution.py:99
  237.9 11.9 %copy.25 = bf16[8,2048,128]{2,0,1:T(8,128)(2,1)S(1)} copy(bf16[8,2048,128]{2,1,0:T(8,128)(2,1)S(1)} %fusion) | data formatting | bytes 8388608 | tf_op jit(solution)/shard_map/convert_element_type | solution.py:99
  249.8 57.1 %all_to_all.33 = bf16[8,2048,128]{2,0,1:T(8,128)(2,1)S(1)} all-to-all(bf16[8,2048,128]{2,0,1:T(8,128)(2,1)S(1)} %copy.25), channel_id=1, replica_groups=mesh['comp'=2,'mr'=64] {'comp','mr'}, dimensions={1} | all-to-all | bytes 8388608 | tf_op jit(solution)/shard_map/all_to_all | solution.py:100
  306.9 1.4 copy.27
  308.3 11.0 %broadcast_multiply_fusion = f32[16,128,512]{2,1,0:T(8,128)} fusion(f32[16,512]{1,0:T(8,128)S(1)} %fusion.34, bf16[16,1024,512]{2,1,0:T(8,128)(2,1)} %param.7, bf16[1024,16,128]{2,1,0:T(8,128)(2,1)S(1)} %bitcast.82), kind=kOutput, calls=%fused_computation.53 | convolution fusion | flops 2148532224 | bytes 25198592 | tf_op jit(solution)/shard_map/rmk,mrn->mkn/dot_general | solution.py:104
  (2 shorter events, 0.0 us)
Async XLA Ops:
  28.2 14.0 %copy-start.2 = (f32[2,2]{1,0:T(2,128)S(1)}, f32[2,2]{1,0:T(2,128)}, u32[]{:S(2)}) copy-start(f32[2,2]{1,0:T(2,128)} %param.9) | copy-start | bytes 52
  28.2 64.9 %all-to-all-start = ((bf16[1024,16,128]{2,1,0:T(8,128)(2,1)}), bf16[1024,16,128]{2,1,0:T(8,128)(2,1)}, u32[]{:S(2)}, u32[]{:S(2)}) async-start(bf16[1024,16,128]{2,1,0:T(8,128)(2,1)} %copy.20), calls=%async_computation | async-start | bytes 8388608 | tf_op jit(solution)/shard_map/all_to_all | solution.py:84
  162.0 23.7 %copy-start = (bf16[16,1024,64]{1,2,0:T(8,128)(2,1)S(1)}, bf16[16,1024,64]{1,2,0:T(8,128)(2,1)}, u32[]{:S(2)}) copy-start(bf16[16,1024,64]{1,2,0:T(8,128)(2,1)} %get-tuple-element.7) | copy-start | bytes 6291460
  162.0 23.7 %copy-start.1 = (bf16[16,1024,64]{1,2,0:T(8,128)(2,1)S(1)}, bf16[16,1024,64]{1,2,0:T(8,128)(2,1)}, u32[]{:S(2)}) copy-start(bf16[16,1024,64]{1,2,0:T(8,128)(2,1)} %get-tuple-element.8) | copy-start | bytes 6291460
where the time goes:
time: 324 us; the launch traced here: 320 us
  matrix products  116 us (36%)
  blocking collectives  57.1 us (18%)
  waiting for transfers between devices  50.7 us (16%)
  other arithmetic  48.6 us (15%)
  local copies, waits for them, and re-layouts  34.1 us (11%)
  starting transfers between devices  12.4 us (4%)
    all_to_all x1, blocking collectives, on_device(): lax.all_to_all(analysis_input, everyone, split_axis=1, concat_axis=0, til...  57.1 us
    all_to_all x1, waiting for transfers between devices, on_device(): lax.all_to_all(synthesized, everyone, split_axis=0, concat_axis=1, tiled=...  50.7 us
    dot_general x1, matrix products, inverse_modes(): jnp.einsum('am,rak->rmk', sine_table, kicked, preferred_element_type=jnp....  23.7 us
    dot_general x1, matrix products, inverse_modes(): jnp.einsum('am,rak->rmk', cosine_table, kicked, preferred_element_type=jn...  21.5 us
    dot_general x1, matrix products, forward_modes(): jnp.einsum('am,rmk->rak', sine_table, radial, preferred_element_type=jnp....  21.4 us
    dot_general x1, matrix products, forward_modes(): jnp.einsum('am,rmk->rak', cosine_table, radial, preferred_element_type=jn...  21.3 us
    dot_general x1, matrix products, on_device(): jnp.einsum('mkn,mrn->rmk', coeffs, radial_basis, preferred_element_type=j...  17.4 us
    cos x2, other arithmetic, rotate(): cosine = jnp.cos(phase_angle)  15.5 us
  transfers between devices with their start and end apart: 1, of which 1 were waited for; matrix products, arithmetic and copies ran while one was open for 1% of the time, Pallas kernels for 0%

commit v1 on v0

--- a/solution.py
+++ b/solution.py
@@ -97,9 +97,15 @@
     back = inverse_modes(cosine_table, sine_table, kicked, planes)
     back = back.reshape(row_count, comp_width * mode_total, 2 * planes)
     analysis_input = (back * weight_rows[:, None, None]).astype(jnp.bfloat16)
-    gathered_modes = lax.all_to_all(
-        analysis_input, everyone, split_axis=1, concat_axis=0, tiled=True
-    )
+
+    def stops_all_read(panel, mesh_ax, dimension_no, array_axis=0):
+        mat_out = lax.psum(1, axis_name=mesh_ax)
+        extra = jnp.stack(jnp.split(panel, mat_out, axis=dimension_no))
+        return jnp.concatenate(
+            lax.all_to_all(extra, axis_name=mesh_ax, split_axis=0, concat_axis=0), axis=array_axis
+        )
+
+    gathered_modes = stops_all_read(analysis_input, everyone, 1)
     evolved = (
         jnp.einsum("rmk,mrn->mkn", gathered_modes, radial_basis, preferred_element_type=jnp.float32)
         * kept_mask[:, None, :]

time: 324 us -> 313 us (0.966)
  local copies, waits for them, and re-layouts: 34.1 us -> 22.6 us
    convert_element_type x1 -> x0, local copies, waits for them, and re-layouts: 11.9 us -> none  [on_device(): analysis_input = (back * weight_rows[:, None, None]).astype(jnp.bfloat16)]
where the time goes in v1:
time: 313 us; the launch traced here: 308 us
  matrix products  116 us (37%)
  blocking collectives  56.8 us (18%)
  waiting for transfers between devices  50.7 us (16%)
  other arithmetic  48.7 us (16%)
  local copies, waits for them, and re-layouts  22.6 us (7%)
  starting transfers between devices  12.3 us (4%)
    all_to_all x1, blocking collectives, stops_all_read(): lax.all_to_all(extra, axis_name=mesh_ax, split_axis=0, concat_axis=0)  56.8 us
    all_to_all x1, waiting for transfers between devices, on_device(): lax.all_to_all(synthesized, everyone, split_axis=0, concat_axis=1, tiled=...  50.7 us
    dot_general x1, matrix products, inverse_modes(): jnp.einsum('am,rak->rmk', sine_table, kicked, preferred_element_type=jnp....  23.6 us
    dot_general x1, matrix products, forward_modes(): jnp.einsum('am,rmk->rak', sine_table, radial, preferred_element_type=jnp....  21.4 us
    dot_general x1, matrix products, forward_modes(): jnp.einsum('am,rmk->rak', cosine_table, radial, preferred_element_type=jn...  21.3 us
    dot_general x1, matrix products, inverse_modes(): jnp.einsum('am,rak->rmk', cosine_table, kicked, preferred_element_type=jn...  21.3 us
    dot_general x1, matrix products, on_device(): jnp.einsum('mkn,mrn->rmk', coeffs, radial_basis, preferred_element_type=j...  17.4 us
    cos x2, other arithmetic, rotate(): cosine = jnp.cos(phase_angle)  15.5 us
  transfers between devices with their start and end apart: 1, of which 1 were waited for; matrix products, arithmetic and copies ran while one was open for 1% of the time, Pallas kernels for 0%

profile of v1, /device:TPU:1, one launch (start us, length us, event | category | flops | bytes accessed | tf_op | source)
XLA Modules:
  0.0 308.4 jit_solution(14576754555061925891)
XLA Ops:
  0.0 0.7 fusion.34
  0.7 0.2 fusion.33
  0.9 3.0 fusion.22
  4.0 17.4 %convert_bitcast_fusion = bf16[1024,16,128]{0,2,1:T(8,128)(2,1)} fusion(bf16[16,1024,512]{2,1,0:T(8,128)(2,1)} %param.7, bf16[16,64,512]{2,1,0:T(8,128)(2,1)S(1)} %get-tuple-element.12, bf16[16,64,512]{2,1,0:T(8,128)(2,1)S(1)} %get-tuple-element.11), kind=kOutput, calls=%fused_computation.30 | convolution fusion | flops 2153775104 | bytes 23068672 | tf_op jit(solution)/shard_map/mkn,mrn->rmk/dot_general | solution.py:74
  21.3 6.9 %copy.146 = bf16[1024,16,128]{2,1,0:T(8,128)(2,1)} copy(bf16[1024,16,128]{0,2,1:T(8,128)(2,1)} %convert_bitcast_fusion) | data formatting | bytes 8388608 | tf_op jit(solution)/shard_map/convert_element_type | solution.py:76
  28.2 0.0 copy-start.2
  28.2 12.3 %all-to-all-start = ((bf16[1024,16,128]{2,1,0:T(8,128)(2,1)}), bf16[1024,16,128]{2,1,0:T(8,128)(2,1)}, u32[]{:S(2)}, u32[]{:S(2)}) async-start(bf16[1024,16,128]{2,1,0:T(8,128)(2,1)} %copy.146), calls=%async_computation | async-start | bytes 8388608 | tf_op jit(solution)/shard_map/all_to_all | solution.py:84
  40.6 0.8 dynamic_slice.6
  41.4 0.8 dynamic_slice.7
  42.1 0.0 copy-done.2
  42.1 0.2 slice_reduce_fusion.1
  42.3 50.7 %all-to-all-done = bf16[1024,16,128]{2,1,0:T(8,128)(2,1)} async-done(((bf16[1024,16,128]{2,1,0:T(8,128)(2,1)}), bf16[1024,16,128]{2,1,0:T(8,128)(2,1)}, u32[]{:S(2)}, u32[]{:S(2)}) %all-to-all-start) | async-done | bytes 4194336 | tf_op jit(solution)/shard_map/all_to_all | solution.py:84
  93.0 2.9 copy.147
  96.0 21.4 %convolution_bitcast_fusion.2 = f32[16,1024,128]{1,2,0:T(8,128)S(1)} fusion(bf16[16,1024,128]{2,1,0:T(8,128)(2,1)S(1)} %bitcast.593), kind=kOutput, calls=%fused_computation.34 | convolution fusion | flops 4311744512 | bytes 12582912 | tf_op jit(solution)/shard_map/am,rmk->rak/dot_general | solution.py:35
  117.4 21.3 %convolution_bitcast_fusion.3 = f32[16,1024,128]{1,2,0:T(8,128)S(1)} fusion(bf16[16,1024,128]{2,1,0:T(8,128)(2,1)S(1)} %bitcast.594), kind=kOutput, calls=%fused_computation.35 | convolution fusion | flops 4311744512 | bytes 12582912 | tf_op jit(solution)/shard_map/am,rmk->rak/dot_general | solution.py:32
  138.7 2.3 multiply_add_fusion
  140.9 15.3 %fusion.14 = (f32[8,2,1024,64]{2,3,1,0:T(8,128)S(1)}, f32[8,2,1024,64]{2,3,1,0:T(8,128)S(1)}) fusion(f32[8,2,1024,64]{2,3,1,0:T(8,128)S(1)} %bitcast.592, f32[8]{0:T(128)S(1)} %dynamic_slice.6, f32[2]{0:T(128)S(1)} %get-tuple-element.6, f32[2]{0:T(128)S(1)} %get-tuple-element.5), kind=kLoop, calls=%fused_computation.37 | loop fusion | flops 5242880 | bytes 12582960 | tf_op jit(solution)/shard_map/cos | solution.py:23
  156.3 5.6 %fusion.5 = (bf16[16,1024,64]{1,2,0:T(8,128)(2,1)}, bf16[16,1024,64]{1,2,0:T(8,128)(2,1)}) fusion(f32[8,2,1024,64]{2,3,1,0:T(8,128)S(1)} %get-tuple-element.14, f32[8,2,1024,64]{2,3,1,0:T(8,128)S(1)} %get-tuple-element.13, f32[16,1024,128]{1,2,0:T(8,128)S(1)} %convolution_bitcast_fusion.2, f32[16,1024,128]{1,2,0:T(8,128)S(1)} %convolution_bitcast_fusion.3), kind=kLoop, calls=%fused_computation.17 | loop fusion | flops 10485760 | bytes 29360128 | tf_op jit(solution)/shard_map/convert
  161.9 0.0 copy-start
  162.0 0.0 copy-start.1
  162.0 23.6 %convolution_bitcast_fusion = f32[16,1024,128]{1,2,0:T(8,128)} fusion(bf16[16,1024,64]{1,2,0:T(8,128)(2,1)} %get-tuple-element.8, bf16[16,1024,64]{1,2,0:T(8,128)(2,1)} %get-tuple-element.7), kind=kOutput, calls=%fused_computation.32 | convolution fusion | flops 4320133120 | bytes 12582912 | tf_op jit(solution)/shard_map/am,rak->rmk/dot_general | solution.py:45
  185.6 0.0 copy-done
  185.6 0.0 copy-done.1
  185.6 21.3 %convolution_bitcast_fusion.1 = f32[16,1024,128]{1,2,0:T(8,128)} fusion(bf16[16,1024,64]{1,2,0:T(8,128)(2,1)S(1)} %copy-done.1, bf16[16,1024,64]{1,2,0:T(8,128)(2,1)S(1)} %copy-done), kind=kOutput, calls=%fused_computation.33 | convolution fusion | flops 4320133120 | bytes 12582912 | tf_op jit(solution)/shard_map/am,rak->rmk/dot_general | solution.py:42
  206.9 10.6 %slice_add_fusion = (f32[16,1024,64]{1,2,0:T(8,128)S(1)}, f32[16,1024,64]{1,2,0:T(8,128)}) fusion(f32[16,1024,128]{1,2,0:T(8,128)} %convolution_bitcast_fusion, f32[16,1024,128]{1,2,0:T(8,128)} %convolution_bitcast_fusion.1), kind=kLoop, calls=%fused_computation.10 | loop fusion | flops 2097152 | bytes 25165824 | tf_op jit(solution)/shard_map/add | solution.py:46
  217.5 6.8 %pad_maximum_fusion = f32[16,1024,128]{1,2,0:T(8,128)} fusion(f32[16,1024,64]{1,2,0:T(8,128)} %get-tuple-element.10, f32[16,1024,64]{1,2,0:T(8,128)S(1)} %get-tuple-element.9), kind=kLoop, calls=%fused_computation | loop fusion | flops 2097152 | bytes 16777216 | tf_op jit(solution)/shard_map/concatenate | solution.py:48
  224.3 9.2 %copy.150 = f32[16,1024,128]{2,1,0:T(8,128)} copy(f32[16,1024,128]{1,2,0:T(8,128)} %pad_maximum_fusion) | data formatting | bytes 16777216 | tf_op jit(solution)/shard_map/concatenate | solution.py:48
  233.6 4.1 %fusion = bf16[8,2048,128]{2,1,0:T(8,128)(2,1)S(1)} fusion(f32[8]{0:T(128)S(1)} %dynamic_slice.7, f32[8,2048,128]{2,1,0:T(8,128)} %bitcast.590), kind=kLoop, calls=%fused_computation.2 | loop fusion | flops 4194304 | bytes 12582944 | tf_op jit(solution)/shard_map/convert_element_type | solution.py:99
  240.1 56.8 %all_to_all.20 = bf16[128,8,16,128]{3,2,1,0:T(8,128)(2,1)S(1)} all-to-all(bf16[128,8,16,128]{3,2,1,0:T(8,128)(2,1)S(1)} %constant_dynamic-update-slice_fusion), channel_id=1, replica_groups=mesh['comp'=2,'mr'=64] {'comp','mr'}, dimensions={0} | all-to-all | bytes 8388608 | tf_op jit(solution)/shard_map/all_to_all | solution.py:105
  296.9 11.0 %broadcast_multiply_fusion = f32[16,128,512]{2,1,0:T(8,128)} fusion(f32[16,512]{1,0:T(8,128)S(1)} %fusion.34, bf16[16,1024,512]{2,1,0:T(8,128)(2,1)} %param.7, bf16[1024,16,128]{2,1,0:T(8,128)(2,1)S(1)} %bitcast.591), kind=kOutput, calls=%fused_computation.53 | convolution fusion | flops 2148532224 | bytes 25198592 | tf_op jit(solution)/shard_map/rmk,mrn->mkn/dot_general | solution.py:110
  (130 shorter events, 1.8 us)
Async XLA Ops:
  28.2 13.9 %copy-start.2 = (f32[2,2]{1,0:T(2,128)S(1)}, f32[2,2]{1,0:T(2,128)}, u32[]{:S(2)}) copy-start(f32[2,2]{1,0:T(2,128)} %param.9) | copy-start | bytes 52
  28.2 64.8 %all-to-all-start = ((bf16[1024,16,128]{2,1,0:T(8,128)(2,1)}), bf16[1024,16,128]{2,1,0:T(8,128)(2,1)}, u32[]{:S(2)}, u32[]{:S(2)}) async-start(bf16[1024,16,128]{2,1,0:T(8,128)(2,1)} %copy.146), calls=%async_computation | async-start | bytes 8388608 | tf_op jit(solution)/shard_map/all_to_all | solution.py:84
  161.9 23.7 %copy-start = (bf16[16,1024,64]{1,2,0:T(8,128)(2,1)S(1)}, bf16[16,1024,64]{1,2,0:T(8,128)(2,1)}, u32[]{:S(2)}) copy-start(bf16[16,1024,64]{1,2,0:T(8,128)(2,1)} %get-tuple-element.7) | copy-start | bytes 6291460
  162.0 23.6 %copy-start.1 = (bf16[16,1024,64]{1,2,0:T(8,128)(2,1)S(1)}, bf16[16,1024,64]{1,2,0:T(8,128)(2,1)}, u32[]{:S(2)}) copy-start(bf16[16,1024,64]{1,2,0:T(8,128)(2,1)} %get-tuple-element.8) | copy-start | bytes 6291460
